TPU v7x, 256 devices: a whole 4x4x8 slice. The times are simulated.
256 devices in a mesh: batch: 128 (over y, z, x), tile: 2 (over core).
Axes of the slice: x: 4, y: 4, z: 8, core: 2. Of those that a mesh axis runs over, the one named last changes fastest.
Arguments:
- first_view: bfloat16 [256, 8192], P('batch'), may hold values from -1500 to 1500
- second_view: bfloat16 [256, 8192], P('batch'), may hold values from -1500 to 1500
Outputs:
- grad_first: bfloat16 [256, 8192], P('batch', 'tile')
- grad_second: bfloat16 [256, 8192], P('batch', 'tile')
All inputs are finite; a program needn't handle non-finite values.
Results may differ from a plain program's by a relative error of at most 0.0043.
Values may be sent and summed in bfloat16 or wider, within the bound.
A program may use at most 64 MiB of HBM per device.

v0:
```python
import jax
import jax.numpy as jnp
from jax import lax
from jax.sharding import PartitionSpec as P

BAND = 16
epsilon = 1e-05
decorrelation = 0.0051


def fold_rows(received, row_count, row_groups, group_size, block_width):
    return (
        received.reshape(row_count, row_groups, group_size, block_width)
        .sum(2)
        .reshape(row_count, row_groups * block_width)
    )


def fold_cols(received, row_count, row_groups, group_size, block_width):
    return (
        received.reshape(row_count, row_groups, group_size, block_width)
        .sum(1)
        .reshape(row_count, group_size * block_width)
    )


def per_device(first_view, second_view):
    row_count, feature_width = first_view.shape
    device_count = lax.axis_size("batch")
    band_index = lax.axis_index("batch")
    tile_index = lax.axis_index("tile")
    total_rows = row_count * device_count
    half_width = feature_width // 2
    first_float = first_view.astype(jnp.float32)
    second_float = second_view.astype(jnp.float32)
    moments = lax.psum(
        (
            jnp.sum(first_float, 0),
            jnp.sum(first_float * first_float, 0),
            jnp.sum(second_float, 0),
            jnp.sum(second_float * second_float, 0),
        ),
        "batch",
    )
    mean_first = moments[0] / total_rows
    inverse_first = lax.rsqrt(moments[1] / total_rows - mean_first * mean_first + epsilon)
    mean_second = moments[2] / total_rows
    inverse_second = lax.rsqrt(moments[3] / total_rows - mean_second * mean_second + epsilon)
    norm_first = ((first_float - mean_first) * inverse_first).astype(jnp.bfloat16)
    norm_second = ((second_float - mean_second) * inverse_second).astype(jnp.bfloat16)
    group_size = BAND
    row_groups = device_count // group_size
    block_rows = feature_width * group_size // device_count
    block_cols = feature_width // (2 * group_size)
    row_band = band_index // group_size
    column_block = band_index % group_size + group_size * tile_index
    send_first = jnp.broadcast_to(
        norm_first.reshape(row_count, row_groups, 1, block_rows),
        (row_count, row_groups, group_size, block_rows),
    ).reshape(row_count, device_count * block_rows)
    picked = lax.dynamic_slice_in_dim(
        norm_second.reshape(row_count, 2, group_size, block_cols), tile_index, 1, 1
    )
    send_second = jnp.broadcast_to(picked, (row_count, row_groups, group_size, block_cols)).reshape(
        row_count, device_count * block_cols
    )
    whole_first, whole_second = (
        lax.all_to_all(send_first, "batch", split_axis=1, concat_axis=0, tiled=True),
        lax.all_to_all(send_second, "batch", split_axis=1, concat_axis=0, tiled=True),
    )
    correlation = (
        lax.dot_general(
            whole_first, whole_second, (((0,), (0,)), ((), ())), preferred_element_type=jnp.float32
        )
        / total_rows
    )
    row_ids = row_band * block_rows + lax.iota(jnp.int32, block_rows)
    col_ids = column_block * block_cols + lax.iota(jnp.int32, block_cols)
    on_diagonal = row_ids[:, None] == col_ids[None, :]
    slope_tile = jnp.where(on_diagonal, correlation - 1.0, decorrelation * correlation).astype(
        jnp.bfloat16
    )
    pull_first = lax.dot_general(
        whole_second, slope_tile, (((1,), (1,)), ((), ())), preferred_element_type=jnp.float32
    )
    pull_second = jnp.dot(whole_first, slope_tile, preferred_element_type=jnp.float32)
    half_start = tile_index * half_width
    norm_first_half = lax.dynamic_slice_in_dim(norm_first, half_start, half_width, 1).astype(
        jnp.float32
    )
    norm_second_half = lax.dynamic_slice_in_dim(norm_second, half_start, half_width, 1).astype(
        jnp.float32
    )
    inverse_first_half = lax.dynamic_slice_in_dim(inverse_first, half_start, half_width, 0)
    inverse_second_half = lax.dynamic_slice_in_dim(inverse_second, half_start, half_width, 0)
    back_first, back_second = (
        lax.all_to_all(pull_first, "batch", split_axis=0, concat_axis=1, tiled=True),
        lax.all_to_all(pull_second, "batch", split_axis=0, concat_axis=1, tiled=True),
    )
    full_first = fold_rows(back_first, row_count, row_groups, group_size, block_rows)
    pull_second_half = fold_cols(back_second, row_count, row_groups, group_size, block_cols)
    pull_first_half = lax.psum_scatter(full_first, "tile", scatter_dimension=1, tiled=True)
    column_sums = lax.psum(
        (
            jnp.sum(pull_first_half * norm_first_half, 0, keepdims=True),
            jnp.sum(pull_second_half * norm_second_half, 0, keepdims=True),
        ),
        "batch",
    )
    stat_first = column_sums[0] / total_rows
    stat_second = column_sums[1] / total_rows
    grad_first = (inverse_first_half * (pull_first_half - norm_first_half * stat_first)).astype(
        jnp.bfloat16
    )
    grad_second = (
        inverse_second_half * (pull_second_half - norm_second_half * stat_second)
    ).astype(jnp.bfloat16)
    return (grad_first, grad_second)


def solution(mesh):
    return jax.shard_map(
        per_device,
        mesh=mesh,
        in_specs=(P("batch", None), P("batch", None)),
        out_specs=(P("batch", "tile"), P("batch", "tile")),
        check_vma=False,
    )
```

profile of v0, /device:TPU:0, one launch (start us, length us, event | category | flops | bytes accessed | tf_op | source)
XLA Modules:
  0.0 1036.5 jit_solution(13418832312192321948)
XLA Ops:
  7.2 0.0 all-reduce.4.cloned.1.call-start
  7.2 1.5 convert_reduce_fusion.1
  8.7 1.5 convert_reduce_fusion
  10.3 0.0 all-reduce.4.cloned.1.call-update
  10.3 217.0 %all-reduce.4.cloned.1.call-done = (f32[8192]{0:T(1024)}, f32[8192]{0:T(1024)}, f32[8192]{0:T(1024)}, f32[8192]{0:T(1024)}) async-done(((f32[8192]{0:T(1024)}, f32[8192]{0:T(1024)}, f32[8192]{0:T(1024)}, f32[8192]{0:T(1024)}), (f32[8192]{0:T(1024)}, f32[8192]{0:T(1024)}, f32[8192]{0:T(1024)}, f32[8192]{0:T(1024)})) %all-reduce.4.cloned.1.call-update) | async-done | bytes 131088 | tf_op jit(solution)/shard_map/psum | solution.py:36
  227.3 0.8 broadcast_multiply_fusion
  228.1 0.8 fusion.11
  228.9 0.1 broadcast_in_dim.15
  229.0 1.3 copy.30
  230.3 10.2 all-to-all-start.1
  240.6 0.8 fusion.13
  241.4 14.9 %all-to-all-done.1 = bf16[2,128,1024]{2,0,1:T(2,128)(2,1)S(1)} async-done(((bf16[2,128,1024]{2,0,1:T(2,128)(2,1)}), bf16[2,128,1024]{2,0,1:T(2,128)(2,1)S(1)}, u32[]{:S(2)}, u32[]{:S(2)}) %all-to-all-start.1) | async-done | bytes 524320 | tf_op jit(solution)/shard_map/all_to_all | solution.py:68
  256.3 0.7 broadcast_in_dim.13
  257.1 6.3 all-to-all-start
  263.4 0.5 copy.31
  264.0 11.5 %all-to-all-done = bf16[2,128,256]{2,0,1:T(2,128)(2,1)S(1)} async-done(((bf16[2,128,256]{2,0,1:T(2,128)(2,1)}), bf16[2,128,256]{2,0,1:T(2,128)(2,1)S(1)}, u32[]{:S(2)}, u32[]{:S(2)}) %all-to-all-start) | async-done | bytes 131104 | tf_op jit(solution)/shard_map/all_to_all | solution.py:69
  275.4 0.4 fusion
  275.8 0.3 fusion.4
  276.2 1.8 copy.32
  278.0 6.2 all-to-all-start.2
  284.1 0.3 fusion.1
  284.5 0.9 copy.34
  285.4 22.4 %all-to-all-done.2 = f32[128,2,1024]{2,1,0:T(2,128)S(1)} async-done(((f32[128,2,1024]{2,1,0:T(2,128)}), f32[128,2,1024]{2,1,0:T(2,128)S(1)}, u32[]{:S(2)}, u32[]{:S(2)}) %all-to-all-start.2) | async-done | bytes 1048608 | tf_op jit(solution)/shard_map/all_to_all | solution.py:97
  307.9 7.0 all-to-all-start.3
  314.8 0.0 reduce-scatter.4.cloned.1.call-start
  314.9 0.2 bitcast_reduce_fusion
  315.1 2.6 copy.38
  317.8 0.0 reduce-scatter.4.cloned.1.call-update
  317.8 10.1 all-to-all-done.3
  327.9 0.1 reduce_sum.78
  328.0 0.1 fusion.19
  328.1 9.0 reduce-scatter.4.cloned.1.call-done
  337.0 2.2 copy.39
  339.2 0.1 fusion.15
  339.3 689.0 %all-reduce = (f32[1,4096]{1,0:T(1,128)S(1)}, f32[1,4096]{1,0:T(1,128)S(1)}) all-reduce(f32[1,4096]{1,0:T(1,128)S(1)} %bitcast.62, f32[1,4096]{1,0:T(1,128)S(1)} %bitcast.60), channel_id=1, replica_groups=mesh['batch'=128,'tile'=2] {'batch'}, use_global_device_ids=true, to_apply=%region_11.12 | all-reduce | flops 8192 | bytes 65536 | tf_op jit(solution)/shard_map/psum | solution.py:103
  1028.3 0.6 fusion.18
  1029.0 0.6 fusion.22
  (10 shorter events, 0.1 us)
Async XLA Ops:
  7.2 220.1 %all-reduce.4.cloned.1.call-start = ((), (), s32[]{:S(2)}) async-start(), calls=%async_computation.6 | async-start | bytes 262144 | tf_op jit(solution)/shard_map/psum | solution.py:36
  230.3 26.0 %all-to-all-start.1 = ((bf16[2,128,1024]{2,0,1:T(2,128)(2,1)}), bf16[2,128,1024]{2,0,1:T(2,128)(2,1)S(1)}, u32[]{:S(2)}, u32[]{:S(2)}) async-start(bf16[2,128,1024]{2,0,1:T(2,128)(2,1)} %copy.30), calls=%async_computation.1 | async-start | bytes 1048576 | tf_op jit(solution)/shard_map/all_to_all | solution.py:68
  257.1 18.4 %all-to-all-start = ((bf16[2,128,256]{2,0,1:T(2,128)(2,1)}), bf16[2,128,256]{2,0,1:T(2,128)(2,1)S(1)}, u32[]{:S(2)}, u32[]{:S(2)}) async-start(bf16[2,128,256]{2,0,1:T(2,128)(2,1)} %bitcast.1), calls=%async_computation | async-start | bytes 262144 | tf_op jit(solution)/shard_map/all_to_all | solution.py:69
  278.0 29.9 %all-to-all-start.2 = ((f32[128,2,1024]{2,1,0:T(2,128)}), f32[128,2,1024]{2,1,0:T(2,128)S(1)}, u32[]{:S(2)}, u32[]{:S(2)}) async-start(f32[128,2,1024]{2,1,0:T(2,128)} %copy.32), calls=%async_computation.2 | async-start | bytes 2097152 | tf_op jit(solution)/shard_map/all_to_all | solution.py:97
  307.9 20.1 %all-to-all-start.3 = ((f32[128,2,256]{2,1,0:T(2,128)}), f32[128,2,256]{2,1,0:T(2,128)S(1)}, u32[]{:S(2)}, u32[]{:S(2)}) async-start(f32[128,2,256]{2,1,0:T(2,128)} %copy.34), calls=%async_computation.3 | async-start | bytes 524288 | tf_op jit(solution)/shard_map/all_to_all | solution.py:98
  314.8 22.2 %reduce-scatter.4.cloned.1.call-start = ((), (), s32[]{:S(2)}) async-start(), calls=%async_computation.5 | async-start | bytes 6291456
Sparse Core Ops, SparseCore 0:
  13.7 213.4 all-reduce.3
  318.4 18.5 reduce-scatter.3
where the time goes:
time: 1040 us
  blocking collectives  689 us (66%)
  waiting for transfers between devices  285 us (27%)
  starting transfers between devices  29.8 us (3%)
  between operations  14.3 us (1%)
    psum x1, blocking collectives, per_device(): lax.psum((jnp.sum(pull_first_half * norm_first_half, 0, keepdims=True), j...  689 us
    psum x1, waiting for transfers between devices, per_device(): lax.psum((jnp.sum(first_float, 0), jnp.sum(first_float * first_float, 0),...  217 us
    all_to_all x1, waiting for transfers between devices, per_device(): lax.all_to_all(pull_first, 'batch', split_axis=0, concat_axis=1, tiled=True)  22.4 us
  transfers between devices with their start and end apart: 6, of which 6 were waited for; matrix products, arithmetic and copies ran while one was open for 1% of the time, Pallas kernels for 0%

commit v1 on v0

--- a/solution.py
+++ b/solution.py
@@ -64,8 +64,17 @@
     send_second = jnp.broadcast_to(picked, (row_count, row_groups, group_size, block_cols)).reshape(
         row_count, device_count * block_cols
     )
+    _arrange_outputs = lambda here_x, comm_axis: jnp.concatenate(
+        lax.all_to_all(
+            jnp.stack(jnp.split(here_x, lax.axis_size(comm_axis), axis=1), axis=0),
+            concat_axis=0,
+            split_axis=0,
+            axis_name=comm_axis,
+        ),
+        axis=0,
+    )
     whole_first, whole_second = (
-        lax.all_to_all(send_first, "batch", split_axis=1, concat_axis=0, tiled=True),
+        _arrange_outputs(send_first, "batch"),
         lax.all_to_all(send_second, "batch", split_axis=1, concat_axis=0, tiled=True),
     )
     correlation = (

time: 1040 us -> 1110 us (1.067)
  local copies, waits for them, and re-layouts: 10.2 us -> 85 us
    unnamed x4 -> x132, local copies, waits for them, and re-layouts: 4.84 us -> 80.8 us
    all_to_all x1, waiting for transfers between devices: 11.5 us -> 0.01 us  [per_device(): lax.all_to_all(send_second, 'batch', split_axis=1, concat_axis=0, tiled=T...]
  transfers between devices with their start and end apart: 6 -> 6, of which waited for: 6 -> 5; matrix products, arithmetic and copies ran while one was open for 1% -> 7% of each run, Pallas kernels for 0% -> 0%
where the time goes in v1:
time: 1110 us
  blocking collectives  689 us (62%)
  waiting for transfers between devices  274 us (25%)
  local copies, waits for them, and re-layouts  85 us (8%)
  starting transfers between devices  37.8 us (3%)
  between operations  14.3 us (1%)
    psum x1, blocking collectives, per_device(): lax.psum((jnp.sum(pull_first_half * norm_first_half, 0, keepdims=True), j...  689 us
    psum x1, waiting for transfers between devices, per_device(): lax.psum((jnp.sum(first_float, 0), jnp.sum(first_float * first_float, 0),...  217 us
    unnamed x132, local copies, waits for them, and re-layouts  80.8 us
    all_to_all x1, waiting for transfers between devices, per_device(): lax.all_to_all(pull_first, 'batch', split_axis=0, concat_axis=1, tiled=True)  23 us
  transfers between devices with their start and end apart: 6, of which 5 were waited for; matrix products, arithmetic and copies ran while one was open for 7% of the time, Pallas kernels for 0%

profile of v1, /device:TPU:0, one launch (start us, length us, event | category | flops | bytes accessed | tf_op | source)
XLA Modules:
  0.0 1108.8 jit_solution(10157285211499366384)
XLA Ops:
  7.2 1.5 convert_reduce_fusion.1
  8.7 1.5 convert_reduce_fusion
  10.3 217.0 %all-reduce.4.cloned.1.call-done = (f32[8192]{0:T(1024)}, f32[8192]{0:T(1024)}, f32[8192]{0:T(1024)}, f32[8192]{0:T(1024)}) async-done(((f32[8192]{0:T(1024)}, f32[8192]{0:T(1024)}, f32[8192]{0:T(1024)}, f32[8192]{0:T(1024)}), (f32[8192]{0:T(1024)}, f32[8192]{0:T(1024)}, f32[8192]{0:T(1024)}, f32[8192]{0:T(1024)})) %all-reduce.4.cloned.1.call-update) | async-done | bytes 131088 | tf_op jit(solution)/shard_map/psum | solution.py:36
  227.3 0.8 broadcast_multiply_fusion
  228.1 0.8 fusion.11
  228.9 0.8 fusion.13
  229.8 0.8 copy.4101
  230.6 10.2 all-to-all-start
  241.4 0.6 constant_dynamic-update-slice_fusion.127
  245.0 0.6 constant_dynamic-update-slice_fusion.121
  247.4 0.6 constant_dynamic-update-slice_fusion.117
  249.2 0.6 constant_dynamic-update-slice_fusion.114
  253.9 0.6 constant_dynamic-update-slice_fusion.106
  255.7 0.6 constant_dynamic-update-slice_fusion.103
  256.9 0.6 constant_dynamic-update-slice_fusion.101
  262.8 0.6 constant_dynamic-update-slice_fusion.91
  265.8 0.6 constant_dynamic-update-slice_fusion.86
  268.8 0.6 constant_dynamic-update-slice_fusion.81
  269.4 0.6 constant_dynamic-update-slice_fusion.80
  271.8 0.6 constant_dynamic-update-slice_fusion.76
  273.0 0.6 constant_dynamic-update-slice_fusion.74
  275.3 0.6 constant_dynamic-update-slice_fusion.70
  278.3 0.6 constant_dynamic-update-slice_fusion.65
  281.9 0.6 constant_dynamic-update-slice_fusion.59
  287.8 0.6 constant_dynamic-update-slice_fusion.49
  288.4 0.6 constant_dynamic-update-slice_fusion.48
  292.0 0.6 constant_dynamic-update-slice_fusion.42
  296.8 0.6 constant_dynamic-update-slice_fusion.34
  299.1 0.6 constant_dynamic-update-slice_fusion.30
  300.3 0.6 constant_dynamic-update-slice_fusion.28
  305.1 0.6 constant_dynamic-update-slice_fusion.20
  305.7 0.6 constant_dynamic-update-slice_fusion.19
  309.3 0.6 constant_dynamic-update-slice_fusion.13
  309.9 0.6 constant_dynamic-update-slice_fusion.12
  317.6 13.8 %all-to-all-start.1 = ((bf16[128,2,1024]{2,1,0:T(2,128)(2,1)}), bf16[128,2,1024]{2,1,0:T(2,128)(2,1)S(1)}, u32[]{:S(2)}, u32[]{:S(2)}) async-start(bf16[128,2,1024]{2,1,0:T(2,128)(2,1)} %constant_dynamic-update-slice_fusion), calls=%async_computation.1 | async-start | bytes 1048576 | tf_op jit(solution)/shard_map/all_to_all | solution.py:68
  331.4 15.3 %all-to-all-done.1 = bf16[128,2,1024]{2,1,0:T(2,128)(2,1)S(1)} async-done(((bf16[128,2,1024]{2,1,0:T(2,128)(2,1)}), bf16[128,2,1024]{2,1,0:T(2,128)(2,1)S(1)}, u32[]{:S(2)}, u32[]{:S(2)}) %all-to-all-start.1) | async-done | bytes 524320 | tf_op jit(solution)/shard_map/all_to_all | solution.py:68
  347.4 1.8 copy.4104
  349.2 6.7 all-to-all-start.2
  356.3 0.9 copy.4107
  357.2 23.0 %all-to-all-done.2 = f32[128,2,1024]{2,1,0:T(2,128)S(1)} async-done(((f32[128,2,1024]{2,1,0:T(2,128)}), f32[128,2,1024]{2,1,0:T(2,128)S(1)}, u32[]{:S(2)}, u32[]{:S(2)}) %all-to-all-start.2) | async-done | bytes 1048608 | tf_op jit(solution)/shard_map/all_to_all | solution.py:106
  380.2 7.0 all-to-all-start.3
  387.4 2.6 copy.4111
  390.1 10.1 all-to-all-done.3
  400.4 9.0 reduce-scatter.4.cloned.1.call-done
  409.3 2.2 copy.4112
  411.6 689.0 %all-reduce = (f32[1,4096]{1,0:T(1,128)S(1)}, f32[1,4096]{1,0:T(1,128)S(1)}) all-reduce(f32[1,4096]{1,0:T(1,128)S(1)} %bitcast.702, f32[1,4096]{1,0:T(1,128)S(1)} %bitcast.700), channel_id=1, replica_groups=mesh['batch'=128,'tile'=2] {'batch'}, use_global_device_ids=true, to_apply=%region_11.12 | all-reduce | flops 8192 | bytes 65536 | tf_op jit(solution)/shard_map/psum | solution.py:112
  1100.7 0.6 fusion.18
  1101.3 0.6 fusion.22
  (126 shorter events, 62.8 us)
Async XLA Ops:
  7.2 220.1 %all-reduce.4.cloned.1.call-start = ((), (), s32[]{:S(2)}) async-start(), calls=%async_computation.6 | async-start | bytes 262144 | tf_op jit(solution)/shard_map/psum | solution.py:36
  230.6 87.0 %all-to-all-start = ((bf16[2,128,256]{2,0,1:T(2,128)(2,1)}), bf16[2,128,256]{2,0,1:T(2,128)(2,1)S(1)}, u32[]{:S(2)}, u32[]{:S(2)}) async-start(bf16[2,128,256]{2,0,1:T(2,128)(2,1)} %copy.4101), calls=%async_computation | async-start | bytes 262144 | tf_op jit(solution)/shard_map/all_to_all | solution.py:78
  317.6 29.1 %all-to-all-start.1 = ((bf16[128,2,1024]{2,1,0:T(2,128)(2,1)}), bf16[128,2,1024]{2,1,0:T(2,128)(2,1)S(1)}, u32[]{:S(2)}, u32[]{:S(2)}) async-start(bf16[128,2,1024]{2,1,0:T(2,128)(2,1)} %constant_dynamic-update-slice_fusion), calls=%async_computation.1 | async-start | bytes 1048576 | tf_op jit(solution)/shard_map/all_to_all | solution.py:68
  349.2 30.9 %all-to-all-start.2 = ((f32[128,2,1024]{2,1,0:T(2,128)}), f32[128,2,1024]{2,1,0:T(2,128)S(1)}, u32[]{:S(2)}, u32[]{:S(2)}) async-start(f32[128,2,1024]{2,1,0:T(2,128)} %copy.4104), calls=%async_computation.2 | async-start | bytes 2097152 | tf_op jit(solution)/shard_map/all_to_all | solution.py:106
  380.2 20.1 %all-to-all-start.3 = ((f32[128,2,256]{2,1,0:T(2,128)}), f32[128,2,256]{2,1,0:T(2,128)S(1)}, u32[]{:S(2)}, u32[]{:S(2)}) async-start(f32[128,2,256]{2,1,0:T(2,128)} %copy.4107), calls=%async_computation.3 | async-start | bytes 524288 | tf_op jit(solution)/shard_map/all_to_all | solution.py:107
  387.2 22.2 %reduce-scatter.4.cloned.1.call-start = ((), (), s32[]{:S(2)}) async-start(), calls=%async_computation.5 | async-start | bytes 6291456
Sparse Core Ops, SparseCore 0:
  13.7 213.4 all-reduce.3
  390.7 18.5 reduce-scatter.3
